TPU v7x, 32 devices: a whole 2x2x4 slice. The times are simulated.
32 devices in a mesh: group: 2 (over x), sample: 16 (over z, y, core).
Axes of the slice: x: 2, y: 2, z: 4, core: 2. Of those that a mesh axis runs over, the one named last changes fastest.
Arguments:
- queries: bfloat16 [32, 3, 64, 128], P(('group', 'sample')), parts along dimension 0, may hold values from -150 to 150
- prefix_keys: bfloat16 [4096, 8, 128], P(('group', 'sample')), parts along dimension 0, may hold values from -5 to 5
- prefix_values: bfloat16 [4096, 8, 128], P(('group', 'sample')), parts along dimension 0, may hold values from -6 to 6
- suffix_keys: bfloat16 [32, 1024, 8, 128], P(('group', 'sample')), parts along dimension 0, may hold values from -7 to 7
- suffix_values: bfloat16 [32, 1024, 8, 128], P(('group', 'sample')), parts along dimension 0, may hold values from -6 to 6
- suffix_lengths: int32 [32], P(('group', 'sample')), parts along dimension 0, may hold values from 0 to 1024, as said below
- new_keys: bfloat16 [32, 3, 8, 128], P(('group', 'sample')), parts along dimension 0, may hold values from -5 to 5
- new_values: bfloat16 [32, 3, 8, 128], P(('group', 'sample')), parts along dimension 0, may hold values from -6 to 6
Outputs:
- attention: float32 [32, 3, 64, 128], P(('group', 'sample')), parts along dimension 0
There are 2 independent parts, one for each index of `group`. A program takes and returns all parts, laid end to end along the dimension named above; each array names one. Nothing has to cross between parts.
Inputs may be any that keep to these rules, and one draw needn't show every extreme that they name: `suffix_lengths`: some sample of every group has exactly 1024 generated tokens.
All inputs are finite; a program needn't handle non-finite values.
Results may differ from a plain program's by a relative error of at most 0.00042.
Values may be sent and summed in bfloat16 or wider, within the bound.
A program may use at most 128 MiB of HBM per device.

v0:
```python
import math

import jax
import jax.numpy as jnp
from jax import lax
from jax.sharding import PartitionSpec as P


def merge_parts(arrived, arrived_logs, own_max, own_sum, own_total):
    largest = jnp.maximum(jnp.max(arrived_logs, axis=0), own_max)
    weights = jnp.exp(arrived_logs - largest[None])
    own_share = jnp.exp(own_max - largest)
    upper = jnp.sum(weights[..., None] * arrived, axis=0) + own_share[..., None] * own_sum
    lower = jnp.sum(weights, axis=0) + own_share * own_total
    return upper / lower[..., None]


def shards(
    queries,
    prefix_keys,
    prefix_values,
    suffix_keys,
    suffix_values,
    suffix_lengths,
    new_keys,
    new_values,
):
    own_count, step_count, head_count, head_dim = queries.shape
    pre_tokens, kv_heads = (prefix_keys.shape[0], prefix_keys.shape[1])
    group_size = head_count // kv_heads
    suffix_size = suffix_keys.shape[1]
    factor = 1.0 / math.sqrt(head_dim)
    gathered = lax.all_gather(queries, "sample", axis=0, tiled=True)
    sample_rows = gathered.shape[0]
    block_rows = math.gcd(sample_rows, 32)
    own_queries = queries.reshape(own_count, step_count, kv_heads, group_size, head_dim)
    suffix_scores = (
        jnp.einsum(
            "sthgd,sphd->sthgp", own_queries, suffix_keys, preferred_element_type=jnp.float32
        )
        * factor
    )
    positions = lax.broadcasted_iota(jnp.int32, (own_count, suffix_size), 1)
    in_range = (positions < suffix_lengths[:, None])[:, None, None, None, :]
    fresh_scores = (
        jnp.einsum("sthgd,sjhd->sthgj", own_queries, new_keys, preferred_element_type=jnp.float32)
        * factor
    )
    step_rows = lax.broadcasted_iota(jnp.int32, (step_count, step_count), 0)
    step_cols = lax.broadcasted_iota(jnp.int32, (step_count, step_count), 1)
    causal = (step_cols <= step_rows)[None, :, None, None, :]
    suffix_scores = jnp.where(in_range, suffix_scores, -jnp.inf)
    fresh_scores = jnp.where(causal, fresh_scores, -jnp.inf)
    own_max = jnp.maximum(jnp.max(suffix_scores, axis=-1), jnp.max(fresh_scores, axis=-1))
    suffix_powers = jnp.where(in_range, jnp.exp(suffix_scores - own_max[..., None]), 0.0)
    fresh_powers = jnp.where(causal, jnp.exp(fresh_scores - own_max[..., None]), 0.0)
    own_total = jnp.sum(suffix_powers, axis=-1) + jnp.sum(fresh_powers, axis=-1)
    own_sum = jnp.einsum(
        "sthgp,sphd->sthgd",
        suffix_powers.astype(jnp.bfloat16),
        suffix_values,
        preferred_element_type=jnp.float32,
    )
    own_sum = own_sum + jnp.einsum(
        "sthgj,sjhd->sthgd",
        fresh_powers.astype(jnp.bfloat16),
        new_values,
        preferred_element_type=jnp.float32,
    )
    device_count = lax.axis_size("sample")
    repeats = device_count // kv_heads
    sub_tokens = pre_tokens // repeats

    def regroup(cache):
        return (
            cache.reshape(repeats, sub_tokens, kv_heads, head_dim)
            .transpose(2, 0, 1, 3)
            .reshape(kv_heads * repeats, sub_tokens, head_dim)
        )

    head_keys, head_values = (
        lax.all_to_all(regroup(prefix_keys), "sample", split_axis=0, concat_axis=0, tiled=True),
        lax.all_to_all(regroup(prefix_values), "sample", split_axis=0, concat_axis=0, tiled=True),
    )
    head_keys = head_keys.reshape(device_count * sub_tokens, head_dim)
    wide_values = head_values.reshape(device_count * sub_tokens, head_dim).astype(jnp.float32)
    my_head = lax.axis_index("sample") // repeats
    head_queries = lax.dynamic_index_in_dim(
        gathered.reshape(sample_rows, step_count, kv_heads, group_size, head_dim),
        my_head,
        2,
        keepdims=False,
    )
    query_blocks = head_queries.reshape(
        sample_rows // block_rows, block_rows, step_count, group_size, head_dim
    )

    def head_block(query_block):
        scores = (
            jnp.einsum("btgd,pd->btgp", query_block, head_keys, preferred_element_type=jnp.float32)
            * factor
        )
        maxima = jnp.max(scores, axis=-1)
        powers = jnp.exp(scores - maxima[..., None])
        totals = jnp.sum(powers, axis=-1)
        sums = jnp.einsum("btgp,pd->btgd", powers, wide_values, precision=lax.Precision.HIGHEST)
        return (sums / totals[..., None], maxima + jnp.log(totals))

    pieces, log_totals = lax.map(head_block, query_blocks)
    pieces = pieces.reshape(sample_rows, step_count, group_size, head_dim)
    log_totals = log_totals.reshape(sample_rows, step_count, group_size)
    arrived, arrived_logs = (
        lax.all_to_all(pieces, "sample", split_axis=0, concat_axis=0, tiled=True),
        lax.all_to_all(log_totals, "sample", split_axis=0, concat_axis=0, tiled=True),
    )
    arrived = arrived.reshape(
        kv_heads, repeats, own_count, step_count, group_size, head_dim
    ).transpose(1, 2, 3, 0, 4, 5)
    arrived_logs = arrived_logs.reshape(
        kv_heads, repeats, own_count, step_count, group_size
    ).transpose(1, 2, 3, 0, 4)
    attention = merge_parts(arrived, arrived_logs, own_max, own_sum, own_total)
    return attention.reshape(own_count, step_count, head_count, head_dim)


def solution(mesh):
    in_specs = (
        P(("group", "sample"), None, None, None),
        P(("group", "sample"), None, None),
        P(("group", "sample"), None, None),
        P(("group", "sample"), None, None, None),
        P(("group", "sample"), None, None, None),
        P(("group", "sample")),
        P(("group", "sample"), None, None, None),
        P(("group", "sample"), None, None, None),
    )
    out_specs = P(("group", "sample"), None, None, None)
    return jax.shard_map(shards, mesh=mesh, in_specs=in_specs, out_specs=out_specs, check_vma=False)
```

profile of v0, /device:TPU:0, one launch (start us, length us, event | category | flops | bytes accessed | tf_op | source)
XLA Modules:
  0.0 76.3 jit_solution(11577202515715220669)
XLA Ops:
  0.0 0.0 copy-start
  0.0 0.0 copy-start.3
  0.0 1.8 %copy.29 = bf16[8,2,64,128]{3,2,1,0:T(8,128)(2,1)} copy(bf16[8,2,64,128]{3,0,2,1:T(8,128)(2,1)} %bitcast.101) | data formatting | bytes 524288 | tf_op jit(solution)/shard_map/transpose | solution.py:77
  1.9 7.4 %all-to-all-start = ((bf16[16,64,128]{2,1,0:T(8,128)(2,1)}), bf16[16,64,128]{2,1,0:T(8,128)(2,1)S(1)}, u32[]{:S(2)}, u32[]{:S(2)}) async-start(bf16[16,64,128]{2,1,0:T(8,128)(2,1)} %bitcast.4), calls=%async_computation | async-start | bytes 524288 | tf_op jit(solution)/shard_map/all_to_all | solution.py:82
  10.0 1.7 %copy.34 = bf16[8,2,64,128]{3,2,1,0:T(8,128)(2,1)} copy(bf16[8,2,64,128]{3,0,2,1:T(8,128)(2,1)} %bitcast.102) | data formatting | bytes 524288 | tf_op jit(solution)/shard_map/transpose | solution.py:77
  11.7 0.0 copy-done.3
  11.7 0.0 copy-start.4
  11.7 3.2 %fusion.53 = (f32[3,8,8]{2,0,1:T(4,128)S(1)}, f32[1,3,8,8,1024]{4,3,1,2,0:T(8,128)}) fusion(bf16[1024,8,128,1]{2,1,0,3:T(8,128)(2,1)} %bitcast.104, pred[1024]{0:T(1024)(128)(4,1)S(1)} %iota_compare_fusion, bf16[1,3,64,128]{3,2,1,0:T(8,128)(2,1)S(1)} %copy-done.3), kind=kOutput, calls=%fused_computation.57 | convolution fusion | flops 50921280 | bytes 2934528 | tf_op jit(solution)/shard_map/sthgd,sphd->sthgp/dot_general | solution.py:38
  14.9 0.0 copy-done.4
  14.9 0.3 fusion.54
  15.2 24.0 %all_gather.3 = bf16[16,3,64,128]{3,2,1,0:T(8,128)(2,1)S(1)} all-gather(bf16[1,3,64,128]{3,2,1,0:T(8,128)(2,1)S(1)} %copy-done.3), channel_id=1, replica_groups=mesh['group'=2,'sample'=16] {'sample'}, dimensions={0}, use_global_device_ids=true | all-gather | bytes 835584 | tf_op jit(solution)/shard_map/all_gather | solution.py:33
  39.1 0.0 all-to-all-done
  39.1 3.5 %all-to-all-start.2 = ((bf16[16,64,128]{2,1,0:T(8,128)(2,1)}), bf16[16,64,128]{2,1,0:T(8,128)(2,1)S(1)}, u32[]{:S(2)}, u32[]{:S(2)}) async-start(bf16[16,64,128]{2,1,0:T(8,128)(2,1)} %bitcast.24), calls=%async_computation.2 | async-start | bytes 524288 | tf_op jit(solution)/shard_map/all_to_all | solution.py:83
  42.7 0.5 fusion.52
  43.2 0.0 copy-start.1
  43.2 1.2 %copy-done.1 = f32[16,3,8,1024]{3,2,1,0:T(8,128)} copy-done((f32[16,3,8,1024]{3,2,1,0:T(8,128)}, f32[16,3,8,1024]{3,2,1,0:T(8,128)S(1)}, u32[]{:S(2)}) %copy-start.1) | copy-done | bytes 1572888
  44.3 0.4 fusion.5
  44.7 0.0 copy-start.2
  44.7 0.6 log_add_fusion
  45.4 7.3 %all-to-all-done.2 = bf16[16,64,128]{2,1,0:T(8,128)(2,1)S(1)} async-done(((bf16[16,64,128]{2,1,0:T(8,128)(2,1)}), bf16[16,64,128]{2,1,0:T(8,128)(2,1)S(1)}, u32[]{:S(2)}, u32[]{:S(2)}) %all-to-all-start.2) | async-done | bytes 262176 | tf_op jit(solution)/shard_map/all_to_all | solution.py:83
  52.7 3.5 %all-to-all-start.1 = ((f32[16,3,8]{2,1,0:T(4,128)}), f32[16,3,8]{2,1,0:T(4,128)S(1)}, u32[]{:S(2)}, u32[]{:S(2)}) async-start(f32[16,3,8]{2,1,0:T(4,128)} %log_add_fusion), calls=%async_computation.1 | async-start | bytes 65536 | tf_op jit(solution)/shard_map/all_to_all | solution.py:114
  56.2 3.1 %fusion.18 = f32[16,3,8,128]{3,2,1,0:T(8,128)} fusion(bf16[1024,128,1,1]{1,0,3,2:T(8,128)(2,1)S(1)} %bitcast.103, f32[16,3,8,1024]{3,2,1,0:T(8,128)} %copy-done.1, f32[16,3,8]{2,1,0:T(4,128)S(1)} %get-tuple-element.29, f32[16,3,8]{2,1,0:T(4,128)S(1)} %fusion.5), kind=kOutput, calls=%fused_computation.12 | convolution fusion | flops 604422144 | bytes 2034688 | tf_op jit(solution)/shard_map/while/body/eval_jaxpr/btgp,pd->btgd/dot_general | solution.py:106
  59.3 3.5 %all-to-all-done.1 = f32[16,3,8]{2,1,0:T(4,128)S(1)} async-done(((f32[16,3,8]{2,1,0:T(4,128)}), f32[16,3,8]{2,1,0:T(4,128)S(1)}, u32[]{:S(2)}, u32[]{:S(2)}) %all-to-all-start.1) | async-done | bytes 1568 | tf_op jit(solution)/shard_map/all_to_all | solution.py:114
  62.8 3.5 %all-to-all-start.3 = ((f32[16,3,8,128]{3,2,1,0:T(8,128)}), f32[16,3,8,128]{3,2,1,0:T(8,128)S(1)}, u32[]{:S(2)}, u32[]{:S(2)}) async-start(f32[16,3,8,128]{3,2,1,0:T(8,128)} %fusion.18), calls=%async_computation.3 | async-start | bytes 393216 | tf_op jit(solution)/shard_map/all_to_all | solution.py:113
  66.3 0.0 copy-done.2
  66.4 0.3 fusion.26
  66.6 0.1 fusion.37
  66.8 0.0 copy-done
  66.8 0.0 copy-start.5
  66.8 0.7 fusion
  67.6 7.7 %all-to-all-done.3 = f32[16,3,8,128]{3,2,1,0:T(8,128)S(1)} async-done(((f32[16,3,8,128]{3,2,1,0:T(8,128)}), f32[16,3,8,128]{3,2,1,0:T(8,128)S(1)}, u32[]{:S(2)}, u32[]{:S(2)}) %all-to-all-start.3) | async-done | bytes 196640 | tf_op jit(solution)/shard_map/all_to_all | solution.py:113
  75.2 0.1 multiply_reduce_fusion
  75.3 0.0 copy-done.5
  75.4 0.3 fusion.22
  75.7 0.6 copy.82
  (6 shorter events, 0.1 us)
Async XLA Ops:
  0.0 66.8 %copy-start = (bf16[1,1024,8,128]{3,2,1,0:T(8,128)(2,1)S(1)}, bf16[1,1024,8,128]{3,2,1,0:T(8,128)(2,1)}, u32[]{:S(2)}) copy-start(bf16[1,1024,8,128]{3,2,1,0:T(8,128)(2,1)} %param.12) | copy-start | bytes 6291460
  0.0 11.7 %copy-start.3 = (bf16[1,3,64,128]{3,2,1,0:T(8,128)(2,1)S(1)}, bf16[1,3,64,128]{3,2,1,0:T(8,128)(2,1)}, u32[]{:S(2)}) copy-start(bf16[1,3,64,128]{3,2,1,0:T(8,128)(2,1)} %param.8) | copy-start | bytes 147460
  1.9 37.3 %all-to-all-start = ((bf16[16,64,128]{2,1,0:T(8,128)(2,1)}), bf16[16,64,128]{2,1,0:T(8,128)(2,1)S(1)}, u32[]{:S(2)}, u32[]{:S(2)}) async-start(bf16[16,64,128]{2,1,0:T(8,128)(2,1)} %bitcast.4), calls=%async_computation | async-start | bytes 524288 | tf_op jit(solution)/shard_map/all_to_all | solution.py:82
  11.7 3.2 %copy-start.4 = (bf16[1,3,8,128]{3,2,1,0:T(8,128)(2,1)S(1)}, bf16[1,3,8,128]{3,2,1,0:T(8,128)(2,1)}, u32[]{:S(2)}) copy-start(bf16[1,3,8,128]{3,2,1,0:T(8,128)(2,1)} %param.14) | copy-start | bytes 18436
  39.1 13.5 %all-to-all-start.2 = ((bf16[16,64,128]{2,1,0:T(8,128)(2,1)}), bf16[16,64,128]{2,1,0:T(8,128)(2,1)S(1)}, u32[]{:S(2)}, u32[]{:S(2)}) async-start(bf16[16,64,128]{2,1,0:T(8,128)(2,1)} %bitcast.24), calls=%async_computation.2 | async-start | bytes 524288 | tf_op jit(solution)/shard_map/all_to_all | solution.py:83
  43.2 1.2 %copy-start.1 = (f32[16,3,8,1024]{3,2,1,0:T(8,128)}, f32[16,3,8,1024]{3,2,1,0:T(8,128)S(1)}, u32[]{:S(2)}) copy-start(f32[16,3,8,1024]{3,2,1,0:T(8,128)S(1)} %get-tuple-element.30) | copy-start | bytes 4718596
  44.7 21.6 %copy-start.2 = (f32[1,3,8,8,1024]{4,3,1,2,0:T(8,128)S(1)}, f32[1,3,8,8,1024]{4,3,1,2,0:T(8,128)}, u32[]{:S(2)}) copy-start(f32[1,3,8,8,1024]{4,3,1,2,0:T(8,128)} %get-tuple-element.32) | copy-start | bytes 2359300
  52.7 10.1 %all-to-all-start.1 = ((f32[16,3,8]{2,1,0:T(4,128)}), f32[16,3,8]{2,1,0:T(4,128)S(1)}, u32[]{:S(2)}, u32[]{:S(2)}) async-start(f32[16,3,8]{2,1,0:T(4,128)} %log_add_fusion), calls=%async_computation.1 | async-start | bytes 65536 | tf_op jit(solution)/shard_map/all_to_all | solution.py:114
  62.8 12.5 %all-to-all-start.3 = ((f32[16,3,8,128]{3,2,1,0:T(8,128)}), f32[16,3,8,128]{3,2,1,0:T(8,128)S(1)}, u32[]{:S(2)}, u32[]{:S(2)}) async-start(f32[16,3,8,128]{3,2,1,0:T(8,128)} %fusion.18), calls=%async_computation.3 | async-start | bytes 393216 | tf_op jit(solution)/shard_map/all_to_all | solution.py:113
  66.8 8.5 %copy-start.5 = (bf16[1,3,8,128]{3,2,1,0:T(8,128)(2,1)S(1)}, bf16[1,3,8,128]{3,2,1,0:T(8,128)(2,1)}, u32[]{:S(2)}) copy-start(bf16[1,3,8,128]{3,2,1,0:T(8,128)(2,1)} %param.15) | copy-start | bytes 18436
where the time goes:
time: 76.9 us; the launch traced here: 76.3 us
  blocking collectives  24 us (31%)
  waiting for transfers between devices  18.4 us (24%)
  starting transfers between devices  18 us (23%)
  matrix products  8.06 us (10%)
  local copies, waits for them, and re-layouts  5.38 us (7%)
  other arithmetic  1.65 us (2%)
  between operations  0.81 us (1%)
    all_gather x1, blocking collectives, shards(): gathered = lax.all_gather(queries, 'sample', axis=0, tiled=True)  24 us
    all_to_all x1, waiting for transfers between devices, shards(): lax.all_to_all(pieces, 'sample', split_axis=0, concat_axis=0, tiled=True)  7.67 us
    all_to_all x1, starting transfers between devices, shards(): lax.all_to_all(regroup(prefix_keys), 'sample', split_axis=0, concat_axis=...  7.41 us
    all_to_all x1, waiting for transfers between devices, shards(): lax.all_to_all(regroup(prefix_values), 'sample', split_axis=0, concat_axi...  7.29 us
    transpose x2, local copies, waits for them, and re-layouts, regroup(): return cache.reshape(repeats, sub_tokens, kv_heads, head_dim).transpose(2...  3.56 us
    all_to_all x1, starting transfers between devices, shards(): lax.all_to_all(regroup(prefix_values), 'sample', split_axis=0, concat_axi...  3.53 us
    all_to_all x1, starting transfers between devices, shards(): lax.all_to_all(pieces, 'sample', split_axis=0, concat_axis=0, tiled=True)  3.52 us
    all_to_all x1, starting transfers between devices, shards(): lax.all_to_all(log_totals, 'sample', split_axis=0, concat_axis=0, tiled=T...  3.5 us
  transfers between devices with their start and end apart: 4, of which 3 were waited for; matrix products, arithmetic and copies ran while one was open for 14% of the time, Pallas kernels for 0%

commit v1 on v0

v1 whole, which is shorter than its diff:
```python
import functools
import math

import jax
import jax.numpy as jnp
from jax import lax
from jax.experimental import pallas as pl
from jax.experimental.pallas import tpu as pltpu
from jax.sharding import PartitionSpec as P

F32, BF16 = jnp.float32, jnp.bfloat16


def rows_of(tiles):
    wide = tiles.astype(F32)
    return wide.reshape(math.prod(wide.shape[:-1]), wide.shape[-1])


def nt_dot(a, b):
    return lax.dot_general(a, b, (((1,), (1,)), ((), ())), preferred_element_type=F32)


def kernel(
    n, group, chunk,
    len_ref, q_hbm, pk_hbm, pv_hbm, sk_hbm, sv_hbm, nk_hbm, nv_hbm,
    out_ref,
    q_own, pk, pv, wide, k_send, v_send, q_all, k_all, v_all, sk, sv, nk, nv, s_own,
    o_send, l_send, o_all, l_all,
    local_sem, suf_sem, q_ss, q_rs, k_ss, k_rs, v_ss, v_rs, o_ss, o_rs, l_ss, l_rs,
):
    steps, kvh, gsize, dim = q_hbm.shape
    per = steps * gsize
    tokens = pk.shape[0] // kvh
    factor = 1.0 / math.sqrt(dim)
    me = lax.axis_index("sample")
    head = lax.rem(me, kvh)
    base = me - head
    chunks = sk.shape[0] // chunk

    def remote(src, dst, ss, rs, dev):
        return pltpu.make_async_remote_copy(
            src_ref=src, dst_ref=dst, send_sem=ss, recv_sem=rs,
            device_id={"sample": dev}, device_id_type=pl.DeviceIdType.MESH,
        )

    local = [
        pltpu.make_async_copy(a, b, local_sem.at[i])
        for i, (a, b) in enumerate(
            [(pk_hbm, pk), (pv_hbm, pv), (q_hbm, q_own), (nk_hbm, nk), (nv_hbm, nv)]
        )
    ]
    for c in local:
        c.start()
    own_q = pltpu.make_async_copy(q_hbm.at[:, head], q_all.at[me], q_rs.at[me])
    own_q.start()
    halves = []
    for i, (a, b) in enumerate([(sk_hbm, sk), (sv_hbm, sv)]):
        for c in range(chunks):
            part = pl.ds(c * chunk, chunk)
            halves.append(
                pltpu.make_async_copy(a.at[part], b.at[part], suf_sem.at[i * chunks + c])
            )
    for c in halves:
        c.start()

    barrier = pltpu.get_barrier_semaphore()

    def greet(d, _):
        pl.semaphore_signal(
            barrier, inc=1, device_id={"sample": lax.rem(me + d, n)},
            device_id_type=pl.DeviceIdType.MESH,
        )
        return 0

    lax.fori_loop(1, n, greet, 0)

    for src, copy, dst, mine in ((pk, local[0], k_send, k_all), (pv, local[1], v_send, v_all)):
        copy.wait()
        wide[...] = src[...].astype(F32)
        for h in range(kvh):
            dst[h] = wide[pl.ds(h, tokens, stride=kvh), :].astype(BF16)
        mine[head] = wide[pl.ds(head, tokens, stride=kvh), :].astype(BF16)

    pl.semaphore_wait(barrier, n - 1)

    def q_copy(d):
        dev = lax.rem(me + d, n)
        return remote(q_hbm.at[:, lax.rem(dev, kvh)], q_all.at[me], q_ss.at[d], q_rs.at[me], dev)

    def kv_copy(d, src, dst, ss, rs):
        hd = lax.rem(head + d, kvh)
        return remote(src.at[hd], dst.at[head], ss.at[d], rs.at[head], base + hd)

    def start(copy):
        def body(d, _):
            copy(d).start()
            return 0
        return body

    k_copy = lambda d: kv_copy(d, k_send, k_all, k_ss, k_rs)
    v_copy = lambda d: kv_copy(d, v_send, v_all, v_ss, v_rs)
    lax.fori_loop(1, n, start(q_copy), 0)
    lax.fori_loop(1, kvh, start(k_copy), 0)
    lax.fori_loop(1, kvh, start(v_copy), 0)

    for c in local[2:]:
        c.wait()
    rows = kvh * per
    q_rows = jnp.concatenate(
        [q_own[t, h].astype(F32) for h in range(kvh) for t in range(steps)], axis=0
    ).astype(BF16)
    length = len_ref[0]
    row = lax.broadcasted_iota(jnp.int32, (rows, 128), 0)
    lane = lax.broadcasted_iota(jnp.int32, (rows, 128), 1)
    lane_head = lax.rem(lane, kvh)
    match = (row >= lane_head * per) & (row < (lane_head + 1) * per)
    bias = jnp.where(match, 0.0, -jnp.inf).astype(F32)
    bias_wide = jnp.concatenate([bias] * (chunk // 128), axis=1)
    token_of = lax.div(lax.broadcasted_iota(jnp.int32, (8, chunk), 1), kvh)

    top = jnp.full((rows, 1), -jnp.inf, F32)
    for c in range(chunks):
        halves[c].wait()
        s = nt_dot(q_rows, sk[c * chunk:(c + 1) * chunk, :]) * factor
        limit = jnp.where(token_of < length - c * (chunk // kvh), 0.0, -jnp.inf).astype(F32)[:1]
        s = s + bias_wide + limit
        s_own[c] = s
        top = jnp.maximum(top, jnp.max(s, axis=-1, keepdims=True))

    pad = jnp.zeros((128 - steps * kvh, dim), F32)
    new_k = jnp.concatenate([nk[j].astype(F32) for j in range(steps)] + [pad], axis=0).astype(BF16)
    new_v = jnp.concatenate([nv[j].astype(F32) for j in range(steps)] + [pad], axis=0).astype(BF16)
    step_of = lax.div(lax.rem(row, per), gsize)
    s_new = nt_dot(q_rows, new_k) * factor + bias
    s_new = jnp.where(lax.div(lane, kvh) <= step_of, s_new, -jnp.inf)
    own_max = jnp.maximum(top, jnp.max(s_new, axis=-1, keepdims=True))
    w_new = jnp.exp(s_new - own_max)
    own_total = jnp.sum(w_new, axis=-1, keepdims=True)
    own_sum = jnp.dot(w_new.astype(BF16), new_v, preferred_element_type=F32)
    for c in range(chunks):
        halves[chunks + c].wait()
        w = jnp.exp(s_own[c] - own_max)
        own_total = own_total + jnp.sum(w, axis=-1, keepdims=True)
        own_sum = own_sum + jnp.dot(
            w.astype(BF16), sv[c * chunk:(c + 1) * chunk, :], preferred_element_type=F32
        )

    own_q.wait()

    def arrive(make, rs):
        def body(d, _):
            make(d, rs).wait_recv()
            return 0
        return body

    def q_in(d, _):
        src = lax.rem(me + d, n)
        return remote(q_hbm.at[:, head], q_all.at[src], q_ss.at[d], q_rs.at[src], src)

    def kv_in(src, dst, ss, rs):
        def make(d, _):
            hd = lax.rem(head + d, kvh)
            return remote(src.at[hd], dst.at[hd], ss.at[d], rs.at[hd], base + hd)
        return make

    lax.fori_loop(1, n, arrive(q_in, None), 0)
    lax.fori_loop(1, kvh, arrive(kv_in(k_send, k_all, k_ss, k_rs), None), 0)
    lax.fori_loop(1, kvh, arrive(kv_in(v_send, v_all, v_ss, v_rs), None), 0)

    diag_row = lax.broadcasted_iota(jnp.int32, (per, 128), 0)
    diag_lane = lax.broadcasted_iota(jnp.int32, (per, 128), 1)
    diag = diag_row == diag_lane

    def out_copy(dev):
        return remote(o_send.at[dev], o_all.at[me], o_ss.at[dev], o_rs.at[me], dev)

    def log_copy(dev):
        return remote(l_send.at[dev], l_all.at[me], l_ss.at[dev], l_rs.at[me], dev)

    keys = k_all[...].reshape(kvh * tokens, dim)
    values = v_all[...].reshape(kvh * tokens, dim)
    groups = n // group

    def block(i, _):
        first = lax.rem(lax.div(me, group) + 1 + i, groups) * group
        q_block = rows_of(q_all[pl.ds(first, group)]).astype(BF16)
        s = nt_dot(q_block, keys) * factor
        m = jnp.max(s, axis=-1, keepdims=True)
        w = jnp.exp(s - m)
        total = jnp.sum(w, axis=-1, keepdims=True)
        high = w.astype(BF16)
        low = (w - high.astype(F32)).astype(BF16)
        sums = jnp.dot(high, values, preferred_element_type=F32) + jnp.dot(
            low, values, preferred_element_type=F32
        )
        o_send[pl.ds(first, group)] = (sums / total).reshape(group, per, dim)
        logs = jnp.broadcast_to(m + jnp.log(total), (group * per, 128)).reshape(group, per, 128)
        l_send[pl.ds(first, group)] = jnp.sum(
            jnp.where(diag[None], logs, 0.0), axis=1, keepdims=True
        )
        for j in range(group):
            dev = first + j

            @pl.when(dev != me)
            def _():
                out_copy(dev).start()
                log_copy(dev).start()

        return 0

    lax.fori_loop(0, groups, block, 0)
    mine_o = pltpu.make_async_copy(o_send.at[me], o_all.at[me], o_rs.at[me])
    mine_l = pltpu.make_async_copy(l_send.at[me], l_all.at[me], l_rs.at[me])
    mine_o.start()
    mine_l.start()

    def drain(d, _):
        q_copy(d).wait_send()
        return 0

    def drain_kv(d, _):
        k_copy(d).wait_send()
        v_copy(d).wait_send()
        return 0

    lax.fori_loop(1, n, drain, 0)
    lax.fori_loop(1, kvh, drain_kv, 0)
    mine_o.wait()
    mine_l.wait()

    def results_in(d, _):
        src = lax.rem(me + d, n)
        remote(o_send.at[src], o_all.at[src], o_ss.at[src], o_rs.at[src], src).wait_recv()
        remote(l_send.at[src], l_all.at[src], l_ss.at[src], l_rs.at[src], src).wait_recv()
        return 0

    lax.fori_loop(1, n, results_in, 0)

    repeats = n // kvh
    logs = jnp.sum(
        jnp.where(diag[None], jnp.broadcast_to(l_all[...], (n, per, 128)), 0.0),
        axis=-1, keepdims=True,
    ).reshape(repeats, rows, 1)
    largest = jnp.maximum(jnp.max(logs, axis=0), own_max)
    weights = jnp.exp(logs - largest[None])
    share = jnp.exp(own_max - largest)
    upper = share * own_sum
    lower = share * own_total
    for r in range(repeats):
        piece = o_all[r * kvh:(r + 1) * kvh].reshape(rows, dim)
        upper = upper + weights[r] * piece
        lower = lower + weights[r]
    result = upper / lower
    for h in range(kvh):
        for t in range(steps):
            at = h * per + t * gsize
            out_ref[t, h] = result[at:at + gsize]

    def drain_out(d, _):
        dev = lax.rem(me + d, n)
        out_copy(dev).wait_send()
        log_copy(dev).wait_send()
        return 0

    lax.fori_loop(1, n, drain_out, 0)


def solution(mesh):
    n = mesh.shape["sample"]

    def shards(queries, pk, pv, sk, sv, lengths, nk, nv):
        _, steps, heads, dim = queries.shape
        tokens, kvh, _ = pk.shape
        gsize = heads // kvh
        suffix = sk.shape[1]
        per = steps * gsize
        group = math.gcd(n, 4)
        chunk = math.gcd(suffix * kvh, 1024)
        chunks = suffix * kvh // chunk
        any_spec = pl.BlockSpec(memory_space=pl.ANY)
        dma = pltpu.SemaphoreType.DMA
        out = pl.pallas_call(
            functools.partial(kernel, n, group, chunk),
            out_shape=jax.ShapeDtypeStruct((steps, kvh, gsize, dim), F32),
            in_specs=[pl.BlockSpec(memory_space=pltpu.SMEM)] + [any_spec] * 7,
            out_specs=pl.BlockSpec(memory_space=pltpu.VMEM),
            scratch_shapes=[
                pltpu.VMEM((steps, kvh, gsize, dim), BF16),
                pltpu.VMEM((tokens * kvh, dim), BF16),
                pltpu.VMEM((tokens * kvh, dim), BF16),
                pltpu.VMEM((tokens * kvh, dim), F32),
                pltpu.VMEM((kvh, tokens, dim), BF16),
                pltpu.VMEM((kvh, tokens, dim), BF16),
                pltpu.VMEM((n, steps, gsize, dim), BF16),
                pltpu.VMEM((kvh, tokens, dim), BF16),
                pltpu.VMEM((kvh, tokens, dim), BF16),
                pltpu.VMEM((suffix * kvh, dim), BF16),
                pltpu.VMEM((suffix * kvh, dim), BF16),
                pltpu.VMEM((steps, kvh, dim), BF16),
                pltpu.VMEM((steps, kvh, dim), BF16),
                pltpu.VMEM((chunks, kvh * per, chunk), F32),
                pltpu.VMEM((n, per, dim), F32),
                pltpu.VMEM((n, 1, 128), F32),
                pltpu.VMEM((n, per, dim), F32),
                pltpu.VMEM((n, 1, 128), F32),
                dma((5,)), dma((2 * chunks,)),
                dma((n,)), dma((n,)), dma((kvh,)), dma((kvh,)), dma((kvh,)), dma((kvh,)),
                dma((n,)), dma((n,)), dma((n,)), dma((n,)),
            ],
            compiler_params=pltpu.CompilerParams(
                collective_id=0, has_side_effects=True, vmem_limit_bytes=48 << 20
            ),
        )(
            lengths,
            queries.reshape(steps, kvh, gsize, dim),
            pk.reshape(tokens * kvh, dim),
            pv.reshape(tokens * kvh, dim),
            sk.reshape(suffix * kvh, dim),
            sv.reshape(suffix * kvh, dim),
            nk.reshape(steps, kvh, dim),
            nv.reshape(steps, kvh, dim),
        )
        return out.reshape(1, steps, heads, dim)

    spread = ("group", "sample")
    four = P(spread, None, None, None)
    three = P(spread, None, None)
    return jax.shard_map(
        shards, mesh=mesh,
        in_specs=(four, three, three, four, four, P(spread), four, four),
        out_specs=four, check_vma=False,
    )
```

time: 76.9 us -> 32.2 us (0.42)
  blocking collectives: 24 us -> 0 us
  Pallas kernels: 0 us -> 23.2 us
  waiting for transfers between devices: 18.4 us -> 0 us
  starting transfers between devices: 18 us -> 0 us
  matrix products: 8.06 us -> 0 us
  local copies, waits for them, and re-layouts: 5.38 us -> 7.9 us
  other arithmetic: 1.65 us -> 0 us
    all_gather x1 -> x0, blocking collectives: 24 us -> none  [shards(): gathered = lax.all_gather(queries, 'sample', axis=0, tiled=True)]
    pallas_call x0 -> x1, Pallas kernels: none -> 23.2 us  [shards(): pl.pallas_call(functools.partial(kernel, n, group, chunk), out_shape=jax....]
    all_to_all x4 -> x0, waiting for transfers between devices: 18.4 us -> none  [the longest x1 7.67 us: shards(): lax.all_to_all(pieces, 'sample', split_axis=0, concat_axis=0, tiled=True)]
    all_to_all x4 -> x0, starting transfers between devices: 18 us -> none  [the longest x1 7.41 us: shards(): lax.all_to_all(regroup(prefix_keys), 'sample', split_axis=0, concat_axis=...]
    dot_general x6 -> x0, matrix products: 8.06 us -> none  [the longest x1 3.18 us: shards(): jnp.einsum('sthgd,sphd->sthgp', own_queries, suffix_keys, preferred_eleme...]
    unnamed x12 -> x15, local copies, waits for them, and re-layouts: 1.17 us -> 7.9 us
    transpose x2 -> x0, local copies, waits for them, and re-layouts: 3.56 us -> none  [regroup(): return cache.reshape(repeats, sub_tokens, kv_heads, head_dim).transpose(2...]
    reduce_sum x5 -> x0, other arithmetic: 0.95 us -> none  [the longest x1 0.41 us: head_block(): totals = jnp.sum(powers, axis=-1)]
  transfers between devices with their start and end apart: 4 -> 0, of which waited for: 3 -> 0; matrix products, arithmetic and copies ran while one was open for 14% -> 0% of each run, Pallas kernels for 0% -> 0%
where the time goes in v1:
time: 32.2 us; the launch traced here: 31.8 us
  Pallas kernels  23.2 us (72%)
  local copies, waits for them, and re-layouts  7.9 us (25%)
  between operations  0.67 us (2%)
    pallas_call x1, Pallas kernels, shards(): pl.pallas_call(functools.partial(kernel, n, group, chunk), out_shape=jax....  23.2 us
    unnamed x15, local copies, waits for them, and re-layouts  7.9 us

profile of v1, /device:TPU:0, one launch (start us, length us, event | category | flops | bytes accessed | tf_op | source)
XLA Modules:
  0.0 31.8 jit_solution(15484997894933420224)
XLA Ops:
  0.7 0.0 copy-start
  0.7 1.6 %copy-done = bf16[1,1024,8,128]{3,2,1,0:T(8,128)(2,1)S(1)} copy-done((bf16[1,1024,8,128]{3,2,1,0:T(8,128)(2,1)S(1)}, bf16[1,1024,8,128]{3,2,1,0:T(8,128)(2,1)}, u32[]{:S(2)}) %copy-start) | copy-done | bytes 2097176
  2.2 0.0 copy-start.1
  2.2 1.6 %copy-done.1 = bf16[1,1024,8,128]{3,2,1,0:T(8,128)(2,1)S(1)} copy-done((bf16[1,1024,8,128]{3,2,1,0:T(8,128)(2,1)S(1)}, bf16[1,1024,8,128]{3,2,1,0:T(8,128)(2,1)}, u32[]{:S(2)}) %copy-start.1) | copy-done | bytes 2097176
  3.8 0.0 copy-start.2
  3.8 0.9 %copy-done.2 = bf16[128,8,128]{2,1,0:T(8,128)(2,1)S(1)} copy-done((bf16[128,8,128]{2,1,0:T(8,128)(2,1)S(1)}, bf16[128,8,128]{2,1,0:T(8,128)(2,1)}, u32[]{:S(2)}) %copy-start.2) | copy-done | bytes 262168
  4.8 0.0 copy-start.3
  4.8 0.9 %copy-done.3 = bf16[128,8,128]{2,1,0:T(8,128)(2,1)S(1)} copy-done((bf16[128,8,128]{2,1,0:T(8,128)(2,1)S(1)}, bf16[128,8,128]{2,1,0:T(8,128)(2,1)}, u32[]{:S(2)}) %copy-start.3) | copy-done | bytes 262168
  5.7 0.0 copy-start.4
  5.7 0.8 %copy-done.4 = bf16[1,3,64,128]{3,2,1,0:T(8,128)(2,1)S(1)} copy-done((bf16[1,3,64,128]{3,2,1,0:T(8,128)(2,1)S(1)}, bf16[1,3,64,128]{3,2,1,0:T(8,128)(2,1)}, u32[]{:S(2)}) %copy-start.4) | copy-done | bytes 49176
  6.5 0.0 copy-start.5
  6.5 0.7 %copy-done.5 = bf16[1,3,8,128]{3,2,1,0:T(8,128)(2,1)S(1)} copy-done((bf16[1,3,8,128]{3,2,1,0:T(8,128)(2,1)S(1)}, bf16[1,3,8,128]{3,2,1,0:T(8,128)(2,1)}, u32[]{:S(2)}) %copy-start.5) | copy-done | bytes 6168
  7.2 0.0 copy-start.6
  7.2 0.7 %copy-done.6 = bf16[1,3,8,128]{3,2,1,0:T(8,128)(2,1)S(1)} copy-done((bf16[1,3,8,128]{3,2,1,0:T(8,128)(2,1)S(1)}, bf16[1,3,8,128]{3,2,1,0:T(8,128)(2,1)}, u32[]{:S(2)}) %copy-start.6) | copy-done | bytes 6168
  7.9 23.2 %shard_map.82 = f32[3,8,8,128]{3,2,1,0:T(8,128)S(1)} custom-call(s32[1]{0:T(128)S(6)} %copy.10.len_ref, bf16[3,8,8,128]{3,2,1,0:T(8,128)(2,1)S(1)} %bitcast.13, bf16[1024,128]{1,0:T(8,128)(2,1)S(1)} %bitcast.11, bf16[1024,128]{1,0:T(8,128)(2,1)S(1)} %bitcast.12, bf16[8192,128]{1,0:T(8,128)(2,1)S(1)} %bitcast.8, bf16[8192,128]{1,0:T(8,128)(2,1)S(1)} %bitcast.9, ...), custom_call_target="tpu_custom_call" | custom-call | tf_op jit(solution)/shard_map/pallas_call | solution.py:282
  31.1 0.6 %copy.11 = f32[1,3,64,128]{3,2,1,0:T(8,128)} copy(f32[1,3,64,128]{3,2,1,0:T(8,128)S(1)} %bitcast.10) | data formatting | bytes 196608
Async XLA Ops:
  0.7 1.6 %copy-start = (bf16[1,1024,8,128]{3,2,1,0:T(8,128)(2,1)S(1)}, bf16[1,1024,8,128]{3,2,1,0:T(8,128)(2,1)}, u32[]{:S(2)}) copy-start(bf16[1,1024,8,128]{3,2,1,0:T(8,128)(2,1)} %param.11) | copy-start | bytes 6291460
  2.2 1.6 %copy-start.1 = (bf16[1,1024,8,128]{3,2,1,0:T(8,128)(2,1)S(1)}, bf16[1,1024,8,128]{3,2,1,0:T(8,128)(2,1)}, u32[]{:S(2)}) copy-start(bf16[1,1024,8,128]{3,2,1,0:T(8,128)(2,1)} %param.12) | copy-start | bytes 6291460
  3.8 0.9 %copy-start.2 = (bf16[128,8,128]{2,1,0:T(8,128)(2,1)S(1)}, bf16[128,8,128]{2,1,0:T(8,128)(2,1)}, u32[]{:S(2)}) copy-start(bf16[128,8,128]{2,1,0:T(8,128)(2,1)} %param.9) | copy-start | bytes 786436
  4.8 0.9 %copy-start.3 = (bf16[128,8,128]{2,1,0:T(8,128)(2,1)S(1)}, bf16[128,8,128]{2,1,0:T(8,128)(2,1)}, u32[]{:S(2)}) copy-start(bf16[128,8,128]{2,1,0:T(8,128)(2,1)} %param.10) | copy-start | bytes 786436
  5.7 0.8 %copy-start.4 = (bf16[1,3,64,128]{3,2,1,0:T(8,128)(2,1)S(1)}, bf16[1,3,64,128]{3,2,1,0:T(8,128)(2,1)}, u32[]{:S(2)}) copy-start(bf16[1,3,64,128]{3,2,1,0:T(8,128)(2,1)} %param.8) | copy-start | bytes 147460
  6.5 0.7 %copy-start.5 = (bf16[1,3,8,128]{3,2,1,0:T(8,128)(2,1)S(1)}, bf16[1,3,8,128]{3,2,1,0:T(8,128)(2,1)}, u32[]{:S(2)}) copy-start(bf16[1,3,8,128]{3,2,1,0:T(8,128)(2,1)} %param.14) | copy-start | bytes 18436
  7.2 0.7 %copy-start.6 = (bf16[1,3,8,128]{3,2,1,0:T(8,128)(2,1)S(1)}, bf16[1,3,8,128]{3,2,1,0:T(8,128)(2,1)}, u32[]{:S(2)}) copy-start(bf16[1,3,8,128]{3,2,1,0:T(8,128)(2,1)} %param.15) | copy-start | bytes 18436

commit v2 on v1

--- a/solution.py
+++ b/solution.py
@@ -308,7 +308,7 @@
                 dma((n,)), dma((n,)), dma((n,)), dma((n,)),
             ],
             compiler_params=pltpu.CompilerParams(
-                collective_id=0, has_side_effects=True, vmem_limit_bytes=48 << 20
+                collective_id=0, has_side_effects=True, vmem_limit_bytes=67043328
             ),
         )(
             lengths,

time: 32.2 us -> 26.1 us (0.81)
  local copies, waits for them, and re-layouts: 7.9 us -> 1.54 us
  Pallas kernels: 23.2 us -> 23.7 us
    unnamed x15 -> x1, local copies, waits for them, and re-layouts: 7.9 us -> 1.54 us
    pallas_call x1, Pallas kernels: 23.2 us -> 23.7 us  [shards(): pl.pallas_call(functools.partial(kernel, n, group, chunk), out_shape=jax....]
where the time goes in v2:
time: 26.1 us; the launch traced here: 25.9 us
  Pallas kernels  23.7 us (91%)
  local copies, waits for them, and re-layouts  1.54 us (6%)
  between operations  0.66 us (3%)
    pallas_call x1, Pallas kernels, shards(): pl.pallas_call(functools.partial(kernel, n, group, chunk), out_shape=jax....  23.7 us
    unnamed x1, local copies, waits for them, and re-layouts  1.54 us

profile of v2, /device:TPU:0, one launch (start us, length us, event | category | flops | bytes accessed | tf_op | source)
XLA Modules:
  0.0 25.9 jit_solution(16425538768708452255)
XLA Ops:
  0.7 23.7 %shard_map.82 = f32[3,8,8,128]{3,2,1,0:T(8,128)} custom-call(s32[1]{0:T(128)S(6)} %copy.10.len_ref, bf16[3,8,8,128]{3,2,1,0:T(8,128)(2,1)} %bitcast.13, bf16[1024,128]{1,0:T(8,128)(2,1)} %bitcast.11, bf16[1024,128]{1,0:T(8,128)(2,1)} %bitcast.12, bf16[8192,128]{1,0:T(8,128)(2,1)} %bitcast.8, bf16[8192,128]{1,0:T(8,128)(2,1)} %bitcast.9, ...), custom_call_target="tpu_custom_call" | custom-call | tf_op jit(solution)/shard_map/pallas_call | solution.py:282
  24.4 1.5 %copy.11 = f32[1,3,64,128]{3,2,1,0:T(8,128)} copy(f32[1,3,64,128]{3,2,1,0:T(8,128)} %bitcast.10) | data formatting | bytes 196608

commit v3 on v2

--- a/solution.py
+++ b/solution.py
@@ -22,10 +22,10 @@
 
 def kernel(
     n, group, chunk,
-    len_ref, q_hbm, pk_hbm, pv_hbm, sk_hbm, sv_hbm, nk_hbm, nv_hbm,
+    len_hbm, q_hbm, pk_hbm, pv_hbm, sk_hbm, sv_hbm, nk_hbm, nv_hbm,
     out_ref,
     q_own, pk, pv, wide, k_send, v_send, q_all, k_all, v_all, sk, sv, nk, nv, s_own,
-    o_send, l_send, o_all, l_all,
+    o_send, l_send, o_all, l_all, len_own, w_high, w_low, total_all,
     local_sem, suf_sem, q_ss, q_rs, k_ss, k_rs, v_ss, v_rs, o_ss, o_rs, l_ss, l_rs,
 ):
     steps, kvh, gsize, dim = q_hbm.shape
@@ -46,7 +46,7 @@
     local = [
         pltpu.make_async_copy(a, b, local_sem.at[i])
         for i, (a, b) in enumerate(
-            [(pk_hbm, pk), (pv_hbm, pv), (q_hbm, q_own), (nk_hbm, nk), (nv_hbm, nv)]
+            [(pk_hbm, pk), (pv_hbm, pv), (q_hbm, q_own), (nk_hbm, nk), (nv_hbm, nv), (len_hbm, len_own)]
         )
     ]
     for c in local:
@@ -109,7 +109,7 @@
     q_rows = jnp.concatenate(
         [q_own[t, h].astype(F32) for h in range(kvh) for t in range(steps)], axis=0
     ).astype(BF16)
-    length = len_ref[0]
+    length = len_own[0]
     row = lax.broadcasted_iota(jnp.int32, (rows, 128), 0)
     lane = lax.broadcasted_iota(jnp.int32, (rows, 128), 1)
     lane_head = lax.rem(lane, kvh)
@@ -165,7 +165,6 @@
 
     lax.fori_loop(1, n, arrive(q_in, None), 0)
     lax.fori_loop(1, kvh, arrive(kv_in(k_send, k_all, k_ss, k_rs), None), 0)
-    lax.fori_loop(1, kvh, arrive(kv_in(v_send, v_all, v_ss, v_rs), None), 0)
 
     diag_row = lax.broadcasted_iota(jnp.int32, (per, 128), 0)
     diag_lane = lax.broadcasted_iota(jnp.int32, (per, 128), 1)
@@ -178,33 +177,54 @@
         return remote(l_send.at[dev], l_all.at[me], l_ss.at[dev], l_rs.at[me], dev)
 
     keys = k_all[...].reshape(kvh * tokens, dim)
-    values = v_all[...].reshape(kvh * tokens, dim)
     groups = n // group
-
-    def block(i, _):
-        first = lax.rem(lax.div(me, group) + 1 + i, groups) * group
+    span = group * per
+
+    def first_of(i):
+        return lax.rem(lax.div(me, group) + 1 + i, groups) * group
+
+    def weigh(i, _):
+        first = first_of(i)
+        at = pl.ds(pl.multiple_of(first * per, span), span)
         q_block = rows_of(q_all[pl.ds(first, group)]).astype(BF16)
         s = nt_dot(q_block, keys) * factor
         m = jnp.max(s, axis=-1, keepdims=True)
         w = jnp.exp(s - m)
         total = jnp.sum(w, axis=-1, keepdims=True)
         high = w.astype(BF16)
-        low = (w - high.astype(F32)).astype(BF16)
-        sums = jnp.dot(high, values, preferred_element_type=F32) + jnp.dot(
-            low, values, preferred_element_type=F32
-        )
-        o_send[pl.ds(first, group)] = (sums / total).reshape(group, per, dim)
-        logs = jnp.broadcast_to(m + jnp.log(total), (group * per, 128)).reshape(group, per, 128)
+        w_high[at] = high
+        w_low[at] = (w - high.astype(F32)).astype(BF16)
+        total_all[at] = total
+        logs = jnp.broadcast_to(m + jnp.log(total), (span, 128)).reshape(group, per, 128)
         l_send[pl.ds(first, group)] = jnp.sum(
             jnp.where(diag[None], logs, 0.0), axis=1, keepdims=True
         )
+        for j in range(group):
+            dev = first + j
+
+            @pl.when(dev != me)
+            def _():
+                log_copy(dev).start()
+
+        return 0
+
+    lax.fori_loop(0, groups, weigh, 0)
+    lax.fori_loop(1, kvh, arrive(kv_in(v_send, v_all, v_ss, v_rs), None), 0)
+    values = v_all[...].reshape(kvh * tokens, dim)
+
+    def block(i, _):
+        first = first_of(i)
+        at = pl.ds(pl.multiple_of(first * per, span), span)
+        sums = jnp.dot(w_high[at], values, preferred_element_type=F32) + jnp.dot(
+            w_low[at], values, preferred_element_type=F32
+        )
+        o_send[pl.ds(first, group)] = (sums / total_all[at]).reshape(group, per, dim)
         for j in range(group):
             dev = first + j
 
             @pl.when(dev != me)
             def _():
                 out_copy(dev).start()
-                log_copy(dev).start()
 
         return 0
 
@@ -282,7 +302,7 @@
         out = pl.pallas_call(
             functools.partial(kernel, n, group, chunk),
             out_shape=jax.ShapeDtypeStruct((steps, kvh, gsize, dim), F32),
-            in_specs=[pl.BlockSpec(memory_space=pltpu.SMEM)] + [any_spec] * 7,
+            in_specs=[any_spec] * 8,
             out_specs=pl.BlockSpec(memory_space=pltpu.VMEM),
             scratch_shapes=[
                 pltpu.VMEM((steps, kvh, gsize, dim), BF16),
@@ -303,7 +323,11 @@
                 pltpu.VMEM((n, 1, 128), F32),
                 pltpu.VMEM((n, per, dim), F32),
                 pltpu.VMEM((n, 1, 128), F32),
-                dma((5,)), dma((2 * chunks,)),
+                pltpu.SMEM((1,), jnp.int32),
+                pltpu.VMEM((n * per, kvh * tokens), BF16),
+                pltpu.VMEM((n * per, kvh * tokens), BF16),
+                pltpu.VMEM((n * per, 1), F32),
+                dma((6,)), dma((2 * chunks,)),
                 dma((n,)), dma((n,)), dma((kvh,)), dma((kvh,)), dma((kvh,)), dma((kvh,)),
                 dma((n,)), dma((n,)), dma((n,)), dma((n,)),
             ],

time: 26.1 us -> 25.2 us (0.966)
  Pallas kernels: 23.7 us -> 22.9 us
    pallas_call x1, Pallas kernels: 23.7 us -> 22.9 us  [shards(): pl.pallas_call(functools.partial(kernel, n, group, chunk), out_shape=jax....]
where the time goes in v3:
time: 25.2 us; the launch traced here: 25.1 us
  Pallas kernels  22.9 us (91%)
  local copies, waits for them, and re-layouts  1.54 us (6%)
  between operations  0.66 us (3%)
    pallas_call x1, Pallas kernels, shards(): pl.pallas_call(functools.partial(kernel, n, group, chunk), out_shape=jax....  22.9 us
    unnamed x1, local copies, waits for them, and re-layouts  1.54 us

profile of v3, /device:TPU:0, one launch (start us, length us, event | category | flops | bytes accessed | tf_op | source)
XLA Modules:
  0.0 25.1 jit_solution(3496860313822448809)
XLA Ops:
  0.7 22.9 %shard_map.82 = f32[3,8,8,128]{3,2,1,0:T(8,128)} custom-call(s32[1]{0:T(128)S(6)} %copy.10.len_hbm, bf16[3,8,8,128]{3,2,1,0:T(8,128)(2,1)} %bitcast.13, bf16[1024,128]{1,0:T(8,128)(2,1)} %bitcast.11, bf16[1024,128]{1,0:T(8,128)(2,1)} %bitcast.12, bf16[8192,128]{1,0:T(8,128)(2,1)} %bitcast.8, bf16[8192,128]{1,0:T(8,128)(2,1)} %bitcast.9, ...), custom_call_target="tpu_custom_call" | custom-call | tf_op jit(solution)/shard_map/pallas_call | solution.py:302
  23.5 1.5 %copy.11 = f32[1,3,64,128]{3,2,1,0:T(8,128)} copy(f32[1,3,64,128]{3,2,1,0:T(8,128)} %bitcast.10) | data formatting | bytes 196608

commit v4 on v3

--- a/solution.py
+++ b/solution.py
@@ -25,8 +25,8 @@
     len_hbm, q_hbm, pk_hbm, pv_hbm, sk_hbm, sv_hbm, nk_hbm, nv_hbm,
     out_ref,
     q_own, pk, pv, wide, k_send, v_send, q_all, k_all, v_all, sk, sv, nk, nv, s_own,
-    o_send, l_send, o_all, l_all, len_own, w_high, w_low, total_all,
-    local_sem, suf_sem, q_ss, q_rs, k_ss, k_rs, v_ss, v_rs, o_ss, o_rs, l_ss, l_rs,
+    o_send, l_send, o_all, l_all, len_own, w_high, w_low, total_all, q_far,
+    local_sem, suf_sem, q_ss, q_rs, f_ss, f_rs, k_ss, k_rs, v_ss, v_rs, o_ss, o_rs, l_ss, l_rs,
 ):
     steps, kvh, gsize, dim = q_hbm.shape
     per = steps * gsize
@@ -35,6 +35,8 @@
     me = lax.axis_index("sample")
     head = lax.rem(me, kvh)
     base = me - head
+    blk = lax.div(me, kvh)
+    blocks = n // kvh
     chunks = sk.shape[0] // chunk
 
     def remote(src, dst, ss, rs, dev):
@@ -65,14 +67,19 @@
 
     barrier = pltpu.get_barrier_semaphore()
 
-    def greet(d, _):
+    def greet(dev):
         pl.semaphore_signal(
-            barrier, inc=1, device_id={"sample": lax.rem(me + d, n)},
-            device_id_type=pl.DeviceIdType.MESH,
-        )
-        return 0
-
-    lax.fori_loop(1, n, greet, 0)
+            barrier, inc=1, device_id={"sample": dev}, device_id_type=pl.DeviceIdType.MESH
+        )
+
+    for d in range(1, kvh):
+        greet(base + lax.rem(head + d, kvh))
+
+    def greet_far(e, _):
+        greet(lax.rem(blk + e, blocks) * kvh + head)
+        return 0
+
+    lax.fori_loop(1, blocks, greet_far, 0)
 
     for src, copy, dst, mine in ((pk, local[0], k_send, k_all), (pv, local[1], v_send, v_all)):
         copy.wait()
@@ -81,11 +88,34 @@
             dst[h] = wide[pl.ds(h, tokens, stride=kvh), :].astype(BF16)
         mine[head] = wide[pl.ds(head, tokens, stride=kvh), :].astype(BF16)
 
-    pl.semaphore_wait(barrier, n - 1)
-
-    def q_copy(d):
-        dev = lax.rem(me + d, n)
-        return remote(q_hbm.at[:, lax.rem(dev, kvh)], q_all.at[me], q_ss.at[d], q_rs.at[me], dev)
+    pl.semaphore_wait(barrier, kvh + blocks - 2)
+
+    def far_copy(e):
+        dev = lax.rem(blk + e, blocks) * kvh + head
+        return remote(q_hbm, q_far.at[blk], f_ss.at[e], f_rs.at[blk], dev)
+
+    def far_in(e):
+        r = lax.rem(blk + e, blocks)
+        return remote(q_hbm, q_far.at[r], f_ss.at[e], f_rs.at[r], r * kvh + head)
+
+    def q_copy(e, d):
+        hd = lax.rem(head + d, kvh)
+        r = lax.rem(blk + e, blocks)
+        at = r * kvh + head
+        src = q_hbm if isinstance(e, int) else q_far.at[r]
+        return remote(src.at[:, hd], q_all.at[at], q_ss.at[e * kvh + d], q_rs.at[at], base + hd)
+
+    def q_keep(e):
+        r = lax.rem(blk + e, blocks)
+        at = r * kvh + head
+        return pltpu.make_async_copy(q_far.at[r, :, head], q_all.at[at], q_rs.at[at])
+
+    def q_in(e, d):
+        hd = lax.rem(head + d, kvh)
+        at = lax.rem(blk + e, blocks) * kvh + hd
+        return remote(
+            q_hbm.at[:, head], q_all.at[at], q_ss.at[e * kvh + d], q_rs.at[at], base + hd
+        )
 
     def kv_copy(d, src, dst, ss, rs):
         hd = lax.rem(head + d, kvh)
@@ -99,9 +129,10 @@
 
     k_copy = lambda d: kv_copy(d, k_send, k_all, k_ss, k_rs)
     v_copy = lambda d: kv_copy(d, v_send, v_all, v_ss, v_rs)
-    lax.fori_loop(1, n, start(q_copy), 0)
+    lax.fori_loop(1, blocks, start(far_copy), 0)
+    for d in range(1, kvh):
+        q_copy(0, d).start()
     lax.fori_loop(1, kvh, start(k_copy), 0)
-    lax.fori_loop(1, kvh, start(v_copy), 0)
 
     for c in local[2:]:
         c.wait()
@@ -126,6 +157,16 @@
         s = s + bias_wide + limit
         s_own[c] = s
         top = jnp.maximum(top, jnp.max(s, axis=-1, keepdims=True))
+
+    def hand_on(e, _):
+        far_in(e).wait_recv()
+        for d in range(1, kvh):
+            q_copy(e, d).start()
+        q_keep(e).start()
+        return 0
+
+    lax.fori_loop(1, blocks, hand_on, 0)
+    lax.fori_loop(1, kvh, start(v_copy), 0)
 
     pad = jnp.zeros((128 - steps * kvh, dim), F32)
     new_k = jnp.concatenate([nk[j].astype(F32) for j in range(steps)] + [pad], axis=0).astype(BF16)
@@ -153,17 +194,22 @@
             return 0
         return body
 
-    def q_in(d, _):
-        src = lax.rem(me + d, n)
-        return remote(q_hbm.at[:, head], q_all.at[src], q_ss.at[d], q_rs.at[src], src)
-
     def kv_in(src, dst, ss, rs):
         def make(d, _):
             hd = lax.rem(head + d, kvh)
             return remote(src.at[hd], dst.at[hd], ss.at[d], rs.at[hd], base + hd)
         return make
 
-    lax.fori_loop(1, n, arrive(q_in, None), 0)
+    for d in range(1, kvh):
+        q_in(0, d).wait_recv()
+
+    def far_q_in(e, _):
+        for d in range(1, kvh):
+            q_in(e, d).wait_recv()
+        q_keep(e).wait()
+        return 0
+
+    lax.fori_loop(1, blocks, far_q_in, 0)
     lax.fori_loop(1, kvh, arrive(kv_in(k_send, k_all, k_ss, k_rs), None), 0)
 
     diag_row = lax.broadcasted_iota(jnp.int32, (per, 128), 0)
@@ -181,7 +227,7 @@
     span = group * per
 
     def first_of(i):
-        return lax.rem(lax.div(me, group) + 1 + i, groups) * group
+        return lax.rem(base + kvh + i * group, n)
 
     def weigh(i, _):
         first = first_of(i)
@@ -234,8 +280,13 @@
     mine_o.start()
     mine_l.start()
 
-    def drain(d, _):
-        q_copy(d).wait_send()
+    for d in range(1, kvh):
+        q_copy(0, d).wait_send()
+
+    def drain(e, _):
+        far_copy(e).wait_send()
+        for d in range(1, kvh):
+            q_copy(e, d).wait_send()
         return 0
 
     def drain_kv(d, _):
@@ -243,7 +294,7 @@
         v_copy(d).wait_send()
         return 0
 
-    lax.fori_loop(1, n, drain, 0)
+    lax.fori_loop(1, blocks, drain, 0)
     lax.fori_loop(1, kvh, drain_kv, 0)
     mine_o.wait()
     mine_l.wait()
@@ -294,7 +345,8 @@
         gsize = heads // kvh
         suffix = sk.shape[1]
         per = steps * gsize
-        group = math.gcd(n, 4)
+        group = math.gcd(kvh, 4)
+        blocks = n // kvh
         chunk = math.gcd(suffix * kvh, 1024)
         chunks = suffix * kvh // chunk
         any_spec = pl.BlockSpec(memory_space=pl.ANY)
@@ -327,8 +379,9 @@
                 pltpu.VMEM((n * per, kvh * tokens), BF16),
                 pltpu.VMEM((n * per, kvh * tokens), BF16),
                 pltpu.VMEM((n * per, 1), F32),
+                pltpu.VMEM((blocks, steps, kvh, gsize, dim), BF16),
                 dma((6,)), dma((2 * chunks,)),
-                dma((n,)), dma((n,)), dma((kvh,)), dma((kvh,)), dma((kvh,)), dma((kvh,)),
+                dma((n,)), dma((n,)), dma((blocks,)), dma((blocks,)), dma((kvh,)), dma((kvh,)), dma((kvh,)), dma((kvh,)),
                 dma((n,)), dma((n,)), dma((n,)), dma((n,)),
             ],
             compiler_params=pltpu.CompilerParams(

time: 25.2 us -> 25.5 us (1.012)
    pallas_call x1, Pallas kernels: 22.9 us -> 23.1 us  [shards(): pl.pallas_call(functools.partial(kernel, n, group, chunk), out_shape=jax....]
where the time goes in v4:
time: 25.5 us; the launch traced here: 25.3 us
  Pallas kernels  23.1 us (91%)
  local copies, waits for them, and re-layouts  1.54 us (6%)
  between operations  0.66 us (3%)
    pallas_call x1, Pallas kernels, shards(): pl.pallas_call(functools.partial(kernel, n, group, chunk), out_shape=jax....  23.1 us
    unnamed x1, local copies, waits for them, and re-layouts  1.54 us

profile of v4, /device:TPU:0, one launch (start us, length us, event | category | flops | bytes accessed | tf_op | source)
XLA Modules:
  0.0 25.3 jit_solution(3716049987770080967)
XLA Ops:
  0.7 23.1 %shard_map.82 = f32[3,8,8,128]{3,2,1,0:T(8,128)} custom-call(s32[1]{0:T(128)S(6)} %copy.10.len_hbm, bf16[3,8,8,128]{3,2,1,0:T(8,128)(2,1)} %bitcast.13, bf16[1024,128]{1,0:T(8,128)(2,1)} %bitcast.11, bf16[1024,128]{1,0:T(8,128)(2,1)} %bitcast.12, bf16[8192,128]{1,0:T(8,128)(2,1)} %bitcast.8, bf16[8192,128]{1,0:T(8,128)(2,1)} %bitcast.9, ...), custom_call_target="tpu_custom_call" | custom-call | tf_op jit(solution)/shard_map/pallas_call | solution.py:354
  23.8 1.5 %copy.11 = f32[1,3,64,128]{3,2,1,0:T(8,128)} copy(f32[1,3,64,128]{3,2,1,0:T(8,128)} %bitcast.10) | data formatting | bytes 196608

commit v5 on v3

--- a/solution.py
+++ b/solution.py
@@ -302,7 +302,7 @@
         out = pl.pallas_call(
             functools.partial(kernel, n, group, chunk),
             out_shape=jax.ShapeDtypeStruct((steps, kvh, gsize, dim), F32),
-            in_specs=[any_spec] * 8,
+            in_specs=[any_spec] + [pl.BlockSpec(memory_space=pltpu.HBM)] * 7,
             out_specs=pl.BlockSpec(memory_space=pltpu.VMEM),
             scratch_shapes=[
                 pltpu.VMEM((steps, kvh, gsize, dim), BF16),
@@ -332,10 +332,9 @@
                 dma((n,)), dma((n,)), dma((n,)), dma((n,)),
             ],
             compiler_params=pltpu.CompilerParams(
-                collective_id=0, has_side_effects=True, vmem_limit_bytes=67043328
+                collective_id=0, has_side_effects=True, vmem_limit_bytes=48 << 20
             ),
-        )(
-            lengths,
+        )(lengths, *[pltpu.with_memory_space_constraint(x, pltpu.HBM) for x in (
             queries.reshape(steps, kvh, gsize, dim),
             pk.reshape(tokens * kvh, dim),
             pv.reshape(tokens * kvh, dim),
@@ -343,7 +342,7 @@
             sv.reshape(suffix * kvh, dim),
             nk.reshape(steps, kvh, dim),
             nv.reshape(steps, kvh, dim),
-        )
+        )])
         return out.reshape(1, steps, heads, dim)
 
     spread = ("group", "sample")

time: 25.2 us -> 23.7 us (0.940)
  local copies, waits for them, and re-layouts: 1.54 us -> 0.64 us
  Pallas kernels: 22.9 us -> 22.2 us
    unnamed x1, local copies, waits for them, and re-layouts: 1.54 us -> 0.64 us
    pallas_call x1, Pallas kernels: 22.9 us -> 22.2 us  [shards(): pl.pallas_call(functools.partial(kernel, n, group, chunk), out_shape=jax....]
where the time goes in v5:
time: 23.7 us; the launch traced here: 23.5 us
  Pallas kernels  22.2 us (94%)
  between operations  0.66 us (3%)
  local copies, waits for them, and re-layouts  0.64 us (3%)
    pallas_call x1, Pallas kernels, shards(): pl.pallas_call(functools.partial(kernel, n, group, chunk), out_shape=jax....  22.2 us
    unnamed x1, local copies, waits for them, and re-layouts  0.64 us

profile of v5, /device:TPU:0, one launch (start us, length us, event | category | flops | bytes accessed | tf_op | source)
XLA Modules:
  0.0 23.5 jit_solution(4871845315039084669)
XLA Ops:
  0.7 22.2 %shard_map.82 = f32[3,8,8,128]{3,2,1,0:T(8,128)S(1)} custom-call(s32[1]{0:T(128)S(6)} %copy.10.len_hbm, bf16[3,8,8,128]{3,2,1,0:T(8,128)(2,1)} %bitcast.13, bf16[1024,128]{1,0:T(8,128)(2,1)} %bitcast.11, bf16[1024,128]{1,0:T(8,128)(2,1)} %bitcast.12, bf16[8192,128]{1,0:T(8,128)(2,1)} %bitcast.9, bf16[8192,128]{1,0:T(8,128)(2,1)} %bitcast.10, ...), custom_call_target="tpu_custom_call" | custom-call | tf_op jit(solution)/shard_map/pallas_call | solution.py:302
  22.9 0.6 %copy.11 = f32[1,3,64,128]{3,2,1,0:T(8,128)} copy(f32[1,3,64,128]{3,2,1,0:T(8,128)S(1)} %bitcast.8) | data formatting | bytes 196608

commit v6 on v5

--- a/solution.py
+++ b/solution.py
@@ -181,7 +181,7 @@
     span = group * per
 
     def first_of(i):
-        return lax.rem(lax.div(me, group) + 1 + i, groups) * group
+        return lax.rem(base + kvh + i * group, n)
 
     def weigh(i, _):
         first = first_of(i)

time: 23.7 us -> 23.2 us (0.979)
  Pallas kernels: 22.2 us -> 21.8 us
    pallas_call x1, Pallas kernels: 22.2 us -> 21.8 us  [shards(): pl.pallas_call(functools.partial(kernel, n, group, chunk), out_shape=jax....]
where the time goes in v6:
time: 23.2 us; the launch traced here: 23.1 us
  Pallas kernels  21.8 us (94%)
  between operations  0.66 us (3%)
  local copies, waits for them, and re-layouts  0.64 us (3%)
    pallas_call x1, Pallas kernels, shards(): pl.pallas_call(functools.partial(kernel, n, group, chunk), out_shape=jax....  21.8 us
    unnamed x1, local copies, waits for them, and re-layouts  0.64 us

profile of v6, /device:TPU:0, one launch (start us, length us, event | category | flops | bytes accessed | tf_op | source)
XLA Modules:
  0.0 23.1 jit_solution(9605559242247829420)
XLA Ops:
  0.7 21.8 %shard_map.82 = f32[3,8,8,128]{3,2,1,0:T(8,128)S(1)} custom-call(s32[1]{0:T(128)S(6)} %copy.10.len_hbm, bf16[3,8,8,128]{3,2,1,0:T(8,128)(2,1)} %bitcast.13, bf16[1024,128]{1,0:T(8,128)(2,1)} %bitcast.11, bf16[1024,128]{1,0:T(8,128)(2,1)} %bitcast.12, bf16[8192,128]{1,0:T(8,128)(2,1)} %bitcast.9, bf16[8192,128]{1,0:T(8,128)(2,1)} %bitcast.10, ...), custom_call_target="tpu_custom_call" | custom-call | tf_op jit(solution)/shard_map/pallas_call | solution.py:302
  22.4 0.6 %copy.11 = f32[1,3,64,128]{3,2,1,0:T(8,128)} copy(f32[1,3,64,128]{3,2,1,0:T(8,128)S(1)} %bitcast.8) | data formatting | bytes 196608
